TPU v7x, 32 devices: a whole 2x2x4 slice. The times are simulated.
32 devices in a mesh: enc: 2 (over x), batch: 16 (over z, y, core).
Axes of the slice: x: 2, y: 2, z: 4, core: 2. Of those that a mesh axis runs over, the one named last changes fastest.
Arguments:
- tokens: bfloat16 [2, 16384, 768], P('enc', 'batch'), may hold values from -6 to 6
- cotangent: bfloat16 [2, 16384, 768], P('enc', 'batch'), may hold values from -6 to 6
- projection: bfloat16 [2, 768, 2304], P('enc'), may hold values from -0.21875 to 0.21875
- offsets: bfloat16 [2, 1536], P('enc'), may hold values from -1.1953125 to 1.1953125
- merger: bfloat16 [2, 768, 768], P('enc'), may hold values from -1.75 to 1.75
- adjust: bfloat16 [2, 768], P('enc'), may hold values from -1.1953125 to 1.1953125
- scaling: bfloat16 [2, 768], P('enc'), may hold values from 0.5 to 1.5
- centering: bfloat16 [2, 768], P('enc'), may hold values from -1.1953125 to 1.1953125
- expansion: bfloat16 [2, 768, 3072], P('enc'), may hold values from -0.21875 to 0.21875
- lifting: bfloat16 [2, 3072], P('enc'), may hold values from -1.1953125 to 1.1953125
- contraction: bfloat16 [2, 3072, 768], P('enc'), may hold values from -0.15625 to 0.15625
- settling: bfloat16 [2, 768], P('enc'), may hold values from -1.1953125 to 1.1953125
- rescale: bfloat16 [2, 768], P('enc'), may hold values from 0.5 to 1.5
- recenter: bfloat16 [2, 768], P('enc'), may hold values from -1.1953125 to 1.1953125
- segments: int32 [16384], P('batch'), may hold values from 0 to 15, as said below
- passage_starts: int32 [256], P('batch'), may hold values from 0 to 1023, as said below
- passage_counts: int32 [16], replicated, may hold values from 4 to 16, as said below
- positives: int32 [256], P('batch'), may hold values from 0 to 255, as said below
Outputs:
- encoded: bfloat16 [2, 16384, 768], P('enc', 'batch')
- tokens_gradient: float32 [2, 16384, 768], P('enc', 'batch')
- gradient_projection: float32 [2, 768, 2304], P('enc')
- gradient_offsets: float32 [2, 1536], P('enc')
- gradient_merger: float32 [2, 768, 768], P('enc')
- gradient_adjust: float32 [2, 768], P('enc')
- gradient_scaling: float32 [2, 768], P('enc')
- gradient_centering: float32 [2, 768], P('enc')
- gradient_expansion: float32 [2, 768, 3072], P('enc')
- gradient_lifting: float32 [2, 3072], P('enc')
- gradient_contraction: float32 [2, 3072, 768], P('enc')
- gradient_settling: float32 [2, 768], P('enc')
- gradient_rescale: float32 [2, 768], P('enc')
- gradient_recenter: float32 [2, 768], P('enc')
Inputs may be any that keep to these rules, and one draw needn't show every extreme that they name: `segments`: within one index of batch, passages are runs of consecutive tokens numbered from 0 upward in order; every row of 256 tokens starts a passage and holds 1 to 4 of them; passages start at multiples of 8. `passage_starts`: on each index of batch, slot s below that index's passage count holds the position of passage s's first token; other slots hold arbitrary positions. `passage_counts`: the number of passages on each index of batch; some index holds 16 in every draw. `positives`: A slot i * 16 + s with s below the passage count of index i.
All inputs are finite; a program needn't handle non-finite values.
Results may differ from a plain program's by a relative error of at most 0.014.
Values may be sent and summed in bfloat16 or wider, within the bound.
No kernel may reach another device: no remote copies, remote signals or barrier semaphores. Data moves between devices by JAX's collectives and lax.ppermute only.
A program may use at most 192 MiB of HBM per device.

v0:
```python
import math
import jax
import jax.numpy as jnp
from jax import lax
from jax.sharding import PartitionSpec as P

HEADS = 12
QLEN = 64
BLOCK = 512
EPSILON = 1e-12
SHARPNESS_DIVISOR = 2.0
LOSS_WEIGHT = 2.0
FLOAT_KIND = jnp.float32
BRAIN = jnp.bfloat16


def swapped(value, axis, apart):
    mask = 2**apart
    pairs = [(source, source ^ mask) for source in range(lax.axis_size(axis))]
    return lax.ppermute(value, axis, pairs)


def layer_norm(values, scale_row, shift_row):
    centered = values - jnp.mean(values, axis=-1, keepdims=True)
    spread = jnp.mean(centered * centered, axis=-1, keepdims=True)
    return centered * lax.rsqrt(spread + EPSILON) * scale_row + shift_row


def exact_gelu(values):
    return jax.nn.gelu(values, approximate=False)


def to_low(values):
    return values.astype(BRAIN)


def block_scores(queries, key_rows, block_marks):
    score_scale = 1.0 / math.sqrt(queries.shape[2])
    scores = (
        jnp.einsum("qhd,khd->hqk", queries, key_rows, preferred_element_type=FLOAT_KIND)
        * score_scale
    )
    same_mark = block_marks[:, None] == block_marks[None, :]
    return jnp.where(same_mark[None], scores, -1e30)


def attend_forward(parts):
    queries, key_rows, values, block_marks = parts
    scores = block_scores(queries, key_rows, block_marks)
    row_top = jnp.max(scores, axis=-1, keepdims=True)
    log_total = row_top + jnp.log(jnp.sum(jnp.exp(scores - row_top), axis=-1, keepdims=True))
    weights = to_low(jnp.exp(scores - log_total))
    context = jnp.einsum("hqk,khd->qhd", weights, values, preferred_element_type=FLOAT_KIND)
    return (to_low(context), log_total)


def attend_backward(parts):
    queries, key_rows, values, block_marks, log_total, gradient_context = parts
    score_scale = 1.0 / math.sqrt(queries.shape[2])
    probability = jnp.exp(block_scores(queries, key_rows, block_marks) - log_total)
    gradient_values = jnp.einsum(
        "hqk,qhd->khd", to_low(probability), gradient_context, preferred_element_type=FLOAT_KIND
    )
    gradient_probs = jnp.einsum(
        "qhd,khd->hqk", gradient_context, values, preferred_element_type=FLOAT_KIND
    )
    row_dots = jnp.sum(probability * gradient_probs, axis=-1, keepdims=True)
    gradient_scores = to_low(probability * (gradient_probs - row_dots))
    gradient_queries = (
        jnp.einsum("hqk,khd->qhd", gradient_scores, key_rows, preferred_element_type=FLOAT_KIND)
        * score_scale
    )
    gradient_keys = (
        jnp.einsum("hqk,qhd->khd", gradient_scores, queries, preferred_element_type=FLOAT_KIND)
        * score_scale
    )
    return (gradient_queries, gradient_keys, gradient_values)


def column_sums(values):
    return jnp.sum(values.astype(FLOAT_KIND), axis=0)


def logit_gradients(
    question_row_block, target_row_list, passage_row_block, valid_entries, smoothing_divisor
):
    score_matrix = (
        jnp.einsum(
            "qd,sd->qs", question_row_block, passage_row_block, preferred_element_type=FLOAT_KIND
        )
        * smoothing_divisor
    )
    score_matrix = jnp.where(valid_entries[None, :], score_matrix, -1e30)
    row_top = jnp.max(score_matrix, axis=1, keepdims=True)
    logit_total = row_top + jnp.log(jnp.sum(jnp.exp(score_matrix - row_top), axis=1, keepdims=True))
    probability = jnp.exp(score_matrix - logit_total)
    target_hit = (
        jnp.arange(score_matrix.shape[1], dtype=jnp.int32)[None, :] == target_row_list[:, None]
    )
    return to_low(LOSS_WEIGHT * (probability - target_hit.astype(FLOAT_KIND)))


def shards(
    tokens,
    cotangent,
    projection,
    offsets,
    merger,
    adjust,
    scaling,
    centering,
    expansion,
    lifting,
    contraction,
    settling,
    rescale,
    recenter,
    segments,
    passage_starts,
    passage_counts,
    positives,
):
    enc_index = lax.axis_index("enc")
    is_passage = enc_index == 1
    rows_in = tokens[0]
    row_count, feature_breadth = rows_in.shape
    head_count = HEADS
    head_size = feature_breadth // head_count
    block_count = row_count // BLOCK
    focus_weighting_array = projection[0]
    merge_matrix = merger[0]
    expand_matrix = expansion[0]
    shrink_matrix = contraction[0]
    offset_row = offsets[0].astype(FLOAT_KIND)
    adjust_row = adjust[0].astype(FLOAT_KIND)
    scaling_row = scaling[0].astype(FLOAT_KIND)
    centering_row = centering[0].astype(FLOAT_KIND)
    lifting_row = lifting[0].astype(FLOAT_KIND)
    settling_row = settling[0].astype(FLOAT_KIND)
    rescale_row = rescale[0].astype(FLOAT_KIND)
    recenter_row = recenter[0].astype(FLOAT_KIND)
    position = jnp.arange(row_count, dtype=jnp.int32)
    token_marks = jnp.where(is_passage, segments, position // QLEN)
    block_marks = token_marks.reshape(block_count, BLOCK)
    full_bias = jnp.concatenate(
        [
            offset_row[:feature_breadth],
            jnp.zeros((feature_breadth,), FLOAT_KIND),
            offset_row[feature_breadth:],
        ]
    )
    packed = to_low(
        jnp.dot(rows_in, focus_weighting_array, preferred_element_type=FLOAT_KIND) + full_bias
    )
    parted = packed.reshape(block_count, BLOCK, 3, head_count, head_size)
    queries = parted[:, :, 0]
    key_rows = parted[:, :, 1]
    values = parted[:, :, 2]
    context, log_total = lax.map(attend_forward, (queries, key_rows, values, block_marks))
    context = context.reshape(row_count, feature_breadth)
    attended = jnp.dot(context, merge_matrix, preferred_element_type=FLOAT_KIND) + adjust_row
    normed_one, first_back = jax.vjp(
        layer_norm, rows_in.astype(FLOAT_KIND) + attended, scaling_row, centering_row
    )
    first_low = to_low(normed_one)
    hidden = jnp.dot(first_low, expand_matrix, preferred_element_type=FLOAT_KIND) + lifting_row
    activated = to_low(exact_gelu(hidden))
    shrunk = jnp.dot(activated, shrink_matrix, preferred_element_type=FLOAT_KIND) + settling_row
    encoded, second_back = jax.vjp(layer_norm, normed_one + shrunk, rescale_row, recenter_row)
    encoded_low = to_low(encoded)
    slot_count = passage_starts.shape[0]
    half_count = slot_count // 2
    slot_index = jnp.arange(slot_count, dtype=jnp.int32)
    summary_rows = jnp.where(is_passage, passage_starts, slot_index * QLEN)
    picker = summary_rows[:, None] == position[None, :]
    summary_local = to_low(
        jnp.dot(picker.astype(BRAIN), encoded_low, preferred_element_type=FLOAT_KIND)
    )
    partner = swapped(summary_local, "enc", 0)
    passage_embedding = jnp.where(is_passage, summary_local, partner)
    question_embedding = jnp.where(is_passage, partner, summary_local)
    smoothing_divisor = SHARPNESS_DIVISOR / math.sqrt(feature_breadth)
    valid_entries = (slot_index[None, :] < passage_counts[:, None]).reshape(-1)
    collected_rows = lax.all_gather(passage_embedding, "batch", axis=0, tiled=True)
    local_questions = lax.dynamic_slice_in_dim(
        question_embedding, enc_index * half_count, half_count, 0
    )
    local_targets = lax.dynamic_slice_in_dim(positives, enc_index * half_count, half_count, 0)
    logits_gradient = logit_gradients(
        local_questions, local_targets, collected_rows, valid_entries, smoothing_divisor
    )
    gradient_questions = (
        jnp.dot(logits_gradient, collected_rows, preferred_element_type=FLOAT_KIND)
        * smoothing_divisor
    )
    gradient_passages = lax.psum_scatter(
        jnp.einsum("qs,qd->sd", logits_gradient, local_questions, preferred_element_type=FLOAT_KIND)
        * smoothing_divisor,
        "batch",
        scatter_dimension=0,
        tiled=True,
    )
    back_questions, back_passages = (
        swapped(gradient_questions.astype(jnp.bfloat16), "enc", 0).astype(gradient_questions.dtype),
        swapped(gradient_passages.astype(jnp.bfloat16), "enc", 0).astype(gradient_passages.dtype),
    )
    gradient_summary = jnp.where(
        is_passage,
        gradient_passages + back_passages,
        jnp.concatenate([gradient_questions, back_questions], axis=0),
    )
    gradient_encoded = cotangent[0].astype(FLOAT_KIND) + jnp.einsum(
        "ct,cd->td", picker.astype(FLOAT_KIND), gradient_summary, precision=lax.Precision.HIGHEST
    )
    gradient_two, gradient_rescale, gradient_recenter = second_back(gradient_encoded)
    gradient_shrunk = to_low(gradient_two)
    gradient_settling = column_sums(gradient_shrunk)
    gradient_contraction = jnp.einsum(
        "tf,td->fd", activated, gradient_shrunk, preferred_element_type=FLOAT_KIND
    )
    gradient_activated = jnp.einsum(
        "td,fd->tf", gradient_shrunk, shrink_matrix, preferred_element_type=FLOAT_KIND
    )
    gelu_again, gelu_back = jax.vjp(exact_gelu, hidden)
    gradient_hidden = to_low(gelu_back(gradient_activated)[0])
    gradient_lifting = column_sums(gradient_hidden)
    gradient_expansion = jnp.einsum(
        "td,tf->df", first_low, gradient_hidden, preferred_element_type=FLOAT_KIND
    )
    gradient_first = gradient_two + jnp.einsum(
        "tf,df->td", gradient_hidden, expand_matrix, preferred_element_type=FLOAT_KIND
    )
    gradient_one, gradient_scaling, gradient_centering = first_back(gradient_first)
    gradient_attended = to_low(gradient_one)
    gradient_adjust = column_sums(gradient_attended)
    gradient_merger = jnp.einsum(
        "tc,td->cd", context, gradient_attended, preferred_element_type=FLOAT_KIND
    )
    gradient_context = to_low(
        jnp.einsum("td,cd->tc", gradient_attended, merge_matrix, preferred_element_type=FLOAT_KIND)
    )
    gradient_context = gradient_context.reshape(block_count, BLOCK, head_count, head_size)
    gradient_queries, gradient_keys, gradient_values = lax.map(
        attend_backward, (queries, key_rows, values, block_marks, log_total, gradient_context)
    )
    gradient_packed = to_low(
        jnp.stack([gradient_queries, gradient_keys, gradient_values], axis=2).reshape(
            row_count, 3 * feature_breadth
        )
    )
    packed_sums = column_sums(gradient_packed)
    gradient_offsets = jnp.concatenate(
        [packed_sums[:feature_breadth], packed_sums[2 * feature_breadth :]]
    )
    gradient_projection = jnp.einsum(
        "td,te->de", rows_in, gradient_packed, preferred_element_type=FLOAT_KIND
    )
    tokens_gradient = gradient_one + jnp.einsum(
        "te,de->td", gradient_packed, focus_weighting_array, preferred_element_type=FLOAT_KIND
    )
    every_share = (
        lax.psum_scatter(gradient_projection, "batch", scatter_dimension=0, tiled=True),
        lax.psum_scatter(gradient_offsets, "batch", scatter_dimension=0, tiled=True),
        lax.psum_scatter(gradient_merger, "batch", scatter_dimension=0, tiled=True),
        lax.psum_scatter(gradient_adjust, "batch", scatter_dimension=0, tiled=True),
        lax.psum_scatter(gradient_scaling, "batch", scatter_dimension=0, tiled=True),
        lax.psum_scatter(gradient_centering, "batch", scatter_dimension=0, tiled=True),
        lax.psum_scatter(gradient_expansion, "batch", scatter_dimension=0, tiled=True),
        lax.psum_scatter(gradient_lifting, "batch", scatter_dimension=0, tiled=True),
        lax.psum_scatter(gradient_contraction, "batch", scatter_dimension=0, tiled=True),
        lax.psum_scatter(gradient_settling, "batch", scatter_dimension=0, tiled=True),
        lax.psum_scatter(gradient_rescale, "batch", scatter_dimension=0, tiled=True),
        lax.psum_scatter(gradient_recenter, "batch", scatter_dimension=0, tiled=True),
    )
    overall_aggregate = (
        lax.all_gather(every_share[0].astype(jnp.bfloat16), "batch", axis=0, tiled=True).astype(
            jnp.float32
        ),
        lax.all_gather(every_share[1].astype(jnp.bfloat16), "batch", axis=0, tiled=True).astype(
            jnp.float32
        ),
        lax.all_gather(every_share[2].astype(jnp.bfloat16), "batch", axis=0, tiled=True).astype(
            jnp.float32
        ),
        lax.all_gather(every_share[3].astype(jnp.bfloat16), "batch", axis=0, tiled=True).astype(
            jnp.float32
        ),
        lax.all_gather(every_share[4].astype(jnp.bfloat16), "batch", axis=0, tiled=True).astype(
            jnp.float32
        ),
        lax.all_gather(every_share[5].astype(jnp.bfloat16), "batch", axis=0, tiled=True).astype(
            jnp.float32
        ),
        lax.all_gather(every_share[6].astype(jnp.bfloat16), "batch", axis=0, tiled=True).astype(
            jnp.float32
        ),
        lax.all_gather(every_share[7].astype(jnp.bfloat16), "batch", axis=0, tiled=True).astype(
            jnp.float32
        ),
        lax.all_gather(every_share[8].astype(jnp.bfloat16), "batch", axis=0, tiled=True).astype(
            jnp.float32
        ),
        lax.all_gather(every_share[9].astype(jnp.bfloat16), "batch", axis=0, tiled=True).astype(
            jnp.float32
        ),
        lax.all_gather(every_share[10].astype(jnp.bfloat16), "batch", axis=0, tiled=True).astype(
            jnp.float32
        ),
        lax.all_gather(every_share[11].astype(jnp.bfloat16), "batch", axis=0, tiled=True).astype(
            jnp.float32
        ),
    )
    attend_total = overall_aggregate[:6]
    expand_total = overall_aggregate[6:]
    return (
        to_low(encoded)[None],
        tokens_gradient[None],
        attend_total[0][None],
        attend_total[1][None],
        attend_total[2][None],
        attend_total[3][None],
        attend_total[4][None],
        attend_total[5][None],
        expand_total[0][None],
        expand_total[1][None],
        expand_total[2][None],
        expand_total[3][None],
        expand_total[4][None],
        expand_total[5][None],
    )


def solution(mesh):
    return jax.shard_map(
        shards,
        mesh=mesh,
        in_specs=(
            P("enc", "batch", None),
            P("enc", "batch", None),
            P("enc", None, None),
            P("enc", None),
            P("enc", None, None),
            P("enc", None),
            P("enc", None),
            P("enc", None),
            P("enc", None, None),
            P("enc", None),
            P("enc", None, None),
            P("enc", None),
            P("enc", None),
            P("enc", None),
            P("batch"),
            P("batch"),
            P(),
            P("batch"),
        ),
        out_specs=(
            P("enc", "batch", None),
            P("enc", "batch", None),
            P("enc", None, None),
            P("enc", None),
            P("enc", None, None),
            P("enc", None),
            P("enc", None),
            P("enc", None),
            P("enc", None, None),
            P("enc", None),
            P("enc", None, None),
            P("enc", None),
            P("enc", None),
            P("enc", None),
        ),
        check_vma=False,
    )
```

profile of v0, /device:TPU:0, one launch (start us, length us, event | category | flops | bytes accessed | tf_op | source)
XLA Modules:
  0.0 909.3 jit_solution(17320595831040693999)
XLA Ops:
  14.7 7.3 add_convert_fusion.1
  22.0 6.6 copy.99
  28.6 8.8 reshape.236
  37.4 5.4 slice_bitcast_fusion
  47.3 26.3 %while.26 = (s32[]{:T(128)}, bf16[2,512,12,64]{1,3,2,0:T(8,128)(2,1)}, f32[2,12,512,1]{2,1,3,0:T(8,128)}, bf16[2,512,12,64]{1,3,2,0:T(8,128)(2,1)}, s32[2,512]{1...) while((s32[]{:T(128)}, ...), condition=%wide.region_3.4_spmd, body=%wide.region_0.3_spmd.sunk | while | flops 840558592 | bytes 43204736 | solution.py:159
  47.5 3.5 fusion.135
  51.1 3.5 exponential_reduce_fusion.3
  55.2 5.1 fusion.136
  60.6 3.5 fusion.135
  64.1 3.5 exponential_reduce_fusion.3
  68.3 5.1 fusion.136
  81.7 35.9 %multiply_convert_fusion.1 = (bf16[1024,3072]{1,0:T(8,128)(2,1)}, f32[1024,3072]{1,0:T(8,128)}, f32[1024,3072]{1,0:T(8,128)}) fusion(f32[3072]{0:T(1024)S(1)} %bitcast.227, bf16[1,768,3072]{2,1,0:T(8,128)(2,1)S(1)} %bitcast.233, f32[1024,768]{0,1:T(8,128)S(1)} %get-tuple-element.312, f32[768]{0:T(1024)S(1)} %get-tuple-element.324, ...), kind=kOutput, calls=%fused_computation.63 | convolution fusion | flops 5043388416 | bytes 39348224 | tf_op jit(solution)/shard_map/dot_general | solution.py:166
  117.7 7.7 fusion.99
  127.9 4.3 collective-permute-start
  135.6 22.7 %all_gather.39 = bf16[256,768]{1,0:T(8,128)(2,1)S(1)} all-gather(bf16[16,768]{1,0:T(8,128)(2,1)S(1)} %broadcast_select_fusion), channel_id=1, replica_groups=mesh['enc'=2,'batch'=16] {'batch'}, dimensions={0}, use_global_device_ids=true | all-gather | bytes 417792 | tf_op jit(solution)/shard_map/all_gather | solution.py:184
  162.9 53.9 %reduce-scatter.8.cloned.1.call-done = f32[16,768]{1,0:T(8,128)} async-done(((f32[256,768]{1,0:T(8,128)}), f32[16,768]{1,0:T(8,128)}) %reduce-scatter.8.cloned.1.call-update) | async-done | bytes 49168 | tf_op jit(solution)/shard_map/reduce_scatter | solution.py:196
  226.3 5.8 multiply_reduce_fusion.1
  235.2 19.2 %convert_reduce_fusion = (f32[3072]{0:T(1024)}, bf16[1024,3072]{1,0:T(8,128)(2,1)}) fusion(f32[1024,3072]{1,0:T(8,128)} %get-tuple-element.299, bf16[1024,768]{0,1:T(8,128)(2,1)} %get-tuple-element.289, bf16[1,3072,768]{2,1,0:T(8,128)(2,1)} %param.32, f32[1024,3072]{1,0:T(8,128)} %get-tuple-element.313, f32[3072]{0:T(1024)S(1)} %bitcast.228), kind=kOutput, calls=%fused_computation.61 | convolution fusion | flops 4885312512 | bytes 37773312 | tf_op jit(solution)/shard_map/td,fd->tf/dot_general | solution.py:221
  254.5 11.0 %multiply_reduce_fusion.2 = (f32[768]{0:T(1024)}, f32[1024]{0:T(1024)S(1)}, f32[768]{0:T(1024)}, f32[1024,768]{0,1:T(8,128)S(1)}) fusion(f32[1024,768]{0,1:T(8,128)S(1)} %copy-done.10, f32[1024]{0:T(1024)S(1)} %copy-done.46, f32[1024]{0:T(1024)S(1)} %copy-done.35, f32[768]{0:T(1024)S(1)} %copy-done.42, bf16[1024,3072]{1,0:T(8,128)(2,1)} %get-tuple-element.323, ...), kind=kOutput, calls=%fused_computation.99 | convolution fusion | flops 4839699456 | bytes 20472832 | tf_op jit(solution)/shard_map/tf,df->td/dot_general | solution.py:230
  272.8 4.3 convolution_convert_fusion
  279.8 3.8 reshape.239
  286.5 53.6 %while.27 = (s32[]{:T(128)}, bf16[2,512,12,64]{1,3,2,0:T(8,128)(2,1)}, bf16[2,512,12,64]{1,3,2,0:T(8,128)(2,1)}, bf16[2,512,12,64]{1,3,2,0:T(8,128)(2,1)}, bf16[...) while((s32[]{:T(128)}, ...), condition=%wide.region_17.18_spmd, body=%wide.region_15.17_spmd.sunk | while | flops 2061494272 | bytes 156175728 | solution.py:243
  287.6 3.3 fusion.145
  290.9 3.9 bitcast_dynamic-update-slice_fusion.11
  294.9 6.8 multiply_reduce_fusion.8
  301.7 7.3 multiply_convert_fusion.6
  317.8 3.9 bitcast_dynamic-update-slice_fusion.11
  321.7 6.8 multiply_reduce_fusion.8
  328.5 7.2 multiply_convert_fusion.6
  340.2 5.0 convert_reduce_fusion.1
  345.1 9.4 %copy.112 = bf16[2,512,3,12,64]{1,0,4,3,2:T(2,128)(2,1)} copy(bf16[2,512,3,12,64]{1,4,3,0,2:T(8,128)(2,1)} %get-tuple-element.293) | data formatting | bytes 9437184 | tf_op jit(solution)/shard_map/stack | solution.py:247
  354.6 4.0 copy.127
  360.7 5.8 convolution_bitcast_fusion
  366.5 8.0 copy.124
  374.6 9.9 %fusion.103 = f32[3072,768]{1,0:T(8,128)} fusion(bf16[1024,3072]{1,0:T(8,128)(2,1)} %get-tuple-element.298, bf16[1024,768]{0,1:T(8,128)(2,1)} %get-tuple-element.289), kind=kOutput, calls=%fused_computation.197 | convolution fusion | flops 4831838208 | bytes 17301504 | tf_op jit(solution)/shard_map/tf,td->fd/dot_general | solution.py:218
  385.2 11.3 %fusion.90 = f32[768,3072]{1,0:T(8,128)} fusion(bf16[1024,3072]{1,0:T(8,128)(2,1)} %get-tuple-element.323, f32[1024,768]{0,1:T(8,128)} %copy-done.9, f32[768]{0:T(1024)S(1)} %copy-done.55, f32[768]{0:T(1024)S(1)} %copy-done.43, f32[1024]{0:T(1024)S(1)} %copy-done.47, f32[1024]{0:T(1024)S(1)} %copy-done.36), kind=kOutput, calls=%fused_computation.187 | convolution fusion | flops 4835770368 | bytes 18888704 | tf_op jit(solution)/shard_map/td,tf->df/dot_general | solution.py:227
  398.2 65.3 %reduce-scatter.16.cloned.1.call-done = f32[48,2304]{1,0:T(8,128)} async-done(((f32[768,2304]{1,0:T(8,128)}), f32[48,2304]{1,0:T(8,128)}) %reduce-scatter.16.cloned.1.call-update) | async-done | bytes 442384 | tf_op jit(solution)/shard_map/reduce_scatter | solution.py:262
  465.4 114.2 %reduce-scatter.14.cloned.1.call-done = f32[192,768]{1,0:T(8,128)} async-done(((f32[3072,768]{1,0:T(8,128)}), f32[192,768]{1,0:T(8,128)}) %reduce-scatter.14.cloned.1.call-update) | async-done | bytes 589840 | tf_op jit(solution)/shard_map/reduce_scatter | solution.py:270
  581.4 113.7 %reduce-scatter.12.cloned.1.call-done = f32[48,3072]{1,0:T(8,128)} async-done(((f32[768,3072]{1,0:T(8,128)}), f32[48,3072]{1,0:T(8,128)}) %reduce-scatter.12.cloned.1.call-update) | async-done | bytes 589840 | tf_op jit(solution)/shard_map/reduce_scatter | solution.py:268
  702.3 3.5 fusion.121
  710.5 62.2 %all-reduce.16 = (bf16[1536]{0:T(1024)(128)(2,1)}, bf16[768]{0:T(1024)(128)(2,1)}, bf16[768]{0:T(1024)(128)(2,1)}, bf16[768]{0:T(1024)(128)(2,1)}, bf16[768]{0:T...) all-reduce(f32[1536]{0:T(1024)S(1)} %pad_maximum_fusion.2, ...), channel_id=4, replica_groups=mesh['enc'=2,'batch'=16] {'batch'}, use_global_device_ids=true, to_apply=%region_20.21.clone | all-reduce | flops 9216 | bytes 55296
  789.1 58.6 %all-reduce.17 = (bf16[1536]{0:T(1024)(128)(2,1)}, bf16[768]{0:T(1024)(128)(2,1)}, bf16[768]{0:T(1024)(128)(2,1)}, bf16[768]{0:T(1024)(128)(2,1)}, bf16[768]{0:T...) all-reduce(bf16[1536]{0:T(1024)(128)(2,1)S(1)} %dynamic-update-slic, ...), channel_id=1, replica_groups=mesh['enc'=2,'batch'=16] {'batch'}, use_global_device_ids=true, to_apply=%add | all-reduce | flops 9216 | bytes 36864
  857.8 8.0 add_bitcast_fusion
  865.8 3.5 copy.116
  872.2 5.5 bitcast_convert_fusion.2
  877.7 6.9 bitcast_convert_fusion
  884.6 10.4 %all-gather.9.cloned.1.call-done = bf16[768,3072]{1,0:T(8,128)(2,1)} async-done(((bf16[48,3072]{1,0:T(8,128)(2,1)}), bf16[768,3072]{1,0:T(8,128)(2,1)}) %all-gather.9.cloned.1.call-update) | async-done | bytes 4718608 | tf_op jit(solution)/shard_map/all_gather | solution.py:294
  894.9 7.4 bitcast_convert_fusion.1
  (301 shorter events, 116.9 us)
Async XLA Ops:
  7.2 7.5 copy-start
  7.2 209.6 %reduce-scatter.8.cloned.1.call-start = ((), (), s32[]{:S(2)}) async-start(), calls=%async_computation.5 | async-start | bytes 835584 | tf_op jit(solution)/shard_map/reduce_scatter | solution.py:196
  77.2 4.4 slice-start.2
  77.3 40.4 %slice-start = ((s8[4718592]{0:T(1024)(128)(4,1)}), s8[4194304]{0:T(1024)(128)(4,1)S(1)}, s32[]{:S(2)}) async-start(s8[4718592]{0:T(1024)(128)(4,1)} %bitcast.230), calls=%async_computation.14 | async-start | bytes 8388608
  79.0 38.7 %copy-start.9 = (f32[1024,768]{0,1:T(8,128)}, f32[1024,768]{0,1:T(8,128)S(1)}, u32[]{:S(2)}) copy-start(f32[1024,768]{0,1:T(8,128)S(1)} %get-tuple-element.312) | copy-start | bytes 9437188
  79.0 38.6 %copy-start.34 = (f32[1024]{0:T(1024)}, f32[1024]{0:T(1024)S(1)}, u32[]{:S(2)}) copy-start(f32[1024]{0:T(1024)S(1)} %broadcast_multiply_fusion.1) | copy-start | bytes 12292
  81.6 36.1 %copy-start.45 = (f32[1024]{0:T(1024)}, f32[1024]{0:T(1024)S(1)}, u32[]{:S(2)}) copy-start(f32[1024]{0:T(1024)S(1)} %fusion.85) | copy-start | bytes 12292
  81.6 36.0 %copy-start.41 = (f32[768]{0:T(1024)}, f32[768]{0:T(1024)S(1)}, u32[]{:S(2)}) copy-start(f32[768]{0:T(1024)S(1)} %get-tuple-element.325) | copy-start | bytes 9220
  81.6 36.0 %copy-start.54 = (f32[768]{0:T(1024)}, f32[768]{0:T(1024)S(1)}, u32[]{:S(2)}) copy-start(f32[768]{0:T(1024)S(1)} %get-tuple-element.324) | copy-start | bytes 9220
  81.7 36.0 %copy-start.56 = (f32[768]{0:T(1024)S(1)}, f32[768]{0:T(1024)}, u32[]{:S(2)}) copy-start(f32[768]{0:T(1024)} %convert_reduce_fusion.6) | copy-start | bytes 9220
  81.7 36.0 %slice-start.1 = ((s8[4718592]{0:T(1024)(128)(4,1)}), s8[524288]{0:T(1024)(128)(4,1)S(1)}, s32[]{:S(2)}) async-start(s8[4718592]{0:T(1024)(128)(4,1)} %bitcast.230), calls=%async_computation.15 | async-start | bytes 1048576
  125.5 106.6 %copy-start.23 = (f32[1024]{0:T(1024)}, f32[1024]{0:T(1024)S(1)}, u32[]{:S(2)}) copy-start(f32[1024]{0:T(1024)S(1)} %broadcast_multiply_fusion) | copy-start | bytes 12292
  125.5 6.7 copy-start.64
  126.5 105.6 %copy-start.27 = (f32[1024]{0:T(1024)}, f32[1024]{0:T(1024)S(1)}, u32[]{:S(2)}) copy-start(f32[1024]{0:T(1024)S(1)} %fusion.86) | copy-start | bytes 12292
  126.5 9.0 copy-start.29
  126.6 9.0 copy-start.32
  127.9 6.9 collective-permute-start
  134.8 25.5 %copy-start.61 = (s32[8]{0:T(128)}, s32[8]{0:T(128)S(1)}, u32[]{:S(2)}) copy-start(s32[8]{0:T(128)S(1)} %dynamic_slice.40) | copy-start | bytes 100
  162.9 233.7 %reduce-scatter.10.cloned.1.call-start = ((), (), s32[]{:S(2)}) async-start(), calls=%async_computation.7 | async-start | bytes 2506752 | tf_op jit(solution)/shard_map/reduce_scatter | solution.py:264
  218.2 8.0 collective-permute-start.1
  221.6 4.7 copy-start.30
  221.6 4.0 collective-permute-start.2
  226.3 5.8 copy-start.40
  226.3 5.8 copy-start.4
  235.2 19.3 %copy-start.10 = (f32[1024,768]{0,1:T(8,128)S(1)}, f32[1024,768]{0,1:T(8,128)}, u32[]{:S(2)}) copy-start(f32[1024,768]{0,1:T(8,128)} %copy-done.9) | copy-start | bytes 9437188
  235.2 19.3 %copy-start.35 = (f32[1024]{0:T(1024)S(1)}, f32[1024]{0:T(1024)}, u32[]{:S(2)}) copy-start(f32[1024]{0:T(1024)} %copy-done.34) | copy-start | bytes 12292
  235.2 19.3 %copy-start.42 = (f32[768]{0:T(1024)S(1)}, f32[768]{0:T(1024)}, u32[]{:S(2)}) copy-start(f32[768]{0:T(1024)} %copy-done.41) | copy-start | bytes 9220
  235.2 19.3 %copy-start.46 = (f32[1024]{0:T(1024)S(1)}, f32[1024]{0:T(1024)}, u32[]{:S(2)}) copy-start(f32[1024]{0:T(1024)} %copy-done.45) | copy-start | bytes 12292
  254.5 11.0 %copy-start.38 = (f32[1024]{0:T(1024)S(1)}, f32[1024]{0:T(1024)}, u32[]{:S(2)}) copy-start(f32[1024]{0:T(1024)} %copy-done.37) | copy-start | bytes 12292
  286.5 177.1 %reduce-scatter.16.cloned.1.call-start = ((), (), s32[]{:S(2)}) async-start(), calls=%async_computation.13 | async-start | bytes 7520256 | tf_op jit(solution)/shard_map/reduce_scatter | solution.py:262
  301.7 7.3 copy-start.1
  301.7 7.3 copy-start.19
  328.5 7.2 copy-start.1
  328.5 7.2 copy-start.19
  354.6 6.2 copy-start.14
  374.6 205.0 %reduce-scatter.14.cloned.1.call-start = ((), (), s32[]{:S(2)}) async-start(), calls=%async_computation.11 | async-start | bytes 10027008 | tf_op jit(solution)/shard_map/reduce_scatter | solution.py:270
  384.6 310.6 %reduce-scatter.12.cloned.1.call-start = ((), (), s32[]{:S(2)}) async-start(), calls=%async_computation.9 | async-start | bytes 10027008 | tf_op jit(solution)/shard_map/reduce_scatter | solution.py:268
  396.5 305.7 %copy-start.24 = (f32[1024]{0:T(1024)S(1)}, f32[1024]{0:T(1024)}, u32[]{:S(2)}) copy-start(f32[1024]{0:T(1024)} %copy-done.23) | copy-start | bytes 12292
  396.5 305.7 %copy-start.28 = (f32[1024]{0:T(1024)S(1)}, f32[1024]{0:T(1024)}, u32[]{:S(2)}) copy-start(f32[1024]{0:T(1024)} %copy-done.27) | copy-start | bytes 12292
  396.5 305.7 %copy-start.31 = (f32[768]{0:T(1024)S(1)}, f32[768]{0:T(1024)}, u32[]{:S(2)}) copy-start(f32[768]{0:T(1024)} %copy-done.29) | copy-start | bytes 9220
  396.5 305.7 %copy-start.33 = (f32[768]{0:T(1024)S(1)}, f32[768]{0:T(1024)}, u32[]{:S(2)}) copy-start(f32[768]{0:T(1024)} %copy-done.32) | copy-start | bytes 9220
  396.6 472.8 %all-gather.7.cloned.1.call-start = ((), (), s32[]{:S(2)}) async-start(), calls=%async_computation.8 | async-start | bytes 1253376 | tf_op jit(solution)/shard_map/all_gather | solution.py:282
  398.2 474.0 %all-gather.5.cloned.1.call-start = ((), (), s32[]{:S(2)}) async-start(), calls=%async_computation.6 | async-start | bytes 3760128 | tf_op jit(solution)/shard_map/all_gather | solution.py:276
  465.3 412.4 %all-gather.11.cloned.1.call-start = ((), (), s32[]{:S(2)}) async-start(), calls=%async_computation.12 | async-start | bytes 5013504 | tf_op jit(solution)/shard_map/all_gather | solution.py:300
  581.4 313.5 %all-gather.9.cloned.1.call-start = ((), (), s32[]{:S(2)}) async-start(), calls=%async_computation.10 | async-start | bytes 5013504 | tf_op jit(solution)/shard_map/all_gather | solution.py:294
  782.0 5.4 copy-start.50
  782.8 4.5 copy-start.51
  783.7 4.5 copy-start.52
  (43 other events, 89.8 us)
Sparse Core Ops, SparseCore 0:
  163.0 53.7 reduce-scatter.7
  286.6 61.6 reduce-scatter.9
  374.7 88.8 reduce-scatter.15
  468.7 110.8 reduce-scatter.13
  584.1 111.0 reduce-scatter.11
  697.6 38.2 all-gather.6
  738.5 45.9 all-gather.4
  787.0 52.8 all-gather.10
  843.0 51.9 all-gather.8
where the time goes:
time: 920 us; the launch traced here: 909 us
  waiting for transfers between devices  358 us (39%)
  matrix products  189 us (21%)
  blocking collectives  143 us (16%)
  local copies, waits for them, and re-layouts  115 us (12%)
  other arithmetic  77.7 us (8%)
  between operations  19 us (2%)
    unnamed x2, blocking collectives  121 us
    reduce_scatter x1, waiting for transfers between devices, shards(): lax.psum_scatter(gradient_contraction, 'batch', scatter_dimension=0, tile...  114 us
    reduce_scatter x1, waiting for transfers between devices, shards(): lax.psum_scatter(gradient_expansion, 'batch', scatter_dimension=0, tiled=...  114 us
    reduce_scatter x1, waiting for transfers between devices, shards(): lax.psum_scatter(gradient_projection, 'batch', scatter_dimension=0, tiled...  65.3 us
    reduce_scatter x1, waiting for transfers between devices, shards(): lax.psum_scatter(jnp.einsum('qs,qd->sd', logits_gradient, local_questions...  53.9 us
    unnamed x154, local copies, waits for them, and re-layouts  51.5 us
    dot_general x1, matrix products, shards(): jnp.dot(first_low, expand_matrix, preferred_element_type=FLOAT_KIND)  35.9 us
    all_gather x1, blocking collectives, shards(): lax.all_gather(passage_embedding, 'batch', axis=0, tiled=True)  22.7 us
  transfers between devices with their start and end apart: 12, of which 6 were waited for; matrix products, arithmetic and copies ran while one was open for 20% of the time, Pallas kernels for 0%

commit v1 on v0

--- a/solution.py
+++ b/solution.py
@@ -12,6 +12,35 @@
 LOSS_WEIGHT = 2.0
 FLOAT_KIND = jnp.float32
 BRAIN = jnp.bfloat16
+
+
+def enter_the_row(x0, dimension_no):
+    moved = list(x0.shape[1:])
+    moved[dimension_no] *= x0.shape[0]
+    r2 = jnp.moveaxis(x0, 0, dimension_no).reshape(moved)
+    return r2
+
+
+def proceed_the_grid(incoming_x, axis_tag, dim_k):
+    n_lanes = jax.lax.psum(1, axis_tag)
+    trail = [(t, (t + 1) % n_lanes) for t in range(n_lanes)]
+    x_new, w2 = ([], [])
+    copies = [(nth, u) for u, nth in trail]
+    it = 0
+    while it < n_lanes - 1:
+        if it % 2 == 0:
+            local_next = jax.lax.ppermute(x_new[-1] if x_new else incoming_x, axis_tag, trail)
+            x_new.append(local_next)
+        else:
+            w2.append(jax.lax.ppermute(w2[-1] if w2 else incoming_x, axis_tag, copies))
+        it += 1
+    d_next = jnp.stack([*x_new[::-1], incoming_x, *w2], axis=0)
+    reply = jax.lax.axis_index(axis_tag)
+    item_now = len(x_new)
+    next_value = reply - item_now
+    d_next = d_next[(jnp.arange(n_lanes) - next_value) % n_lanes]
+    work_now = enter_the_row(d_next, dim_k)
+    return work_now
 
 
 def swapped(value, axis, apart):
@@ -181,7 +210,7 @@
     question_embedding = jnp.where(is_passage, partner, summary_local)
     smoothing_divisor = SHARPNESS_DIVISOR / math.sqrt(feature_breadth)
     valid_entries = (slot_index[None, :] < passage_counts[:, None]).reshape(-1)
-    collected_rows = lax.all_gather(passage_embedding, "batch", axis=0, tiled=True)
+    collected_rows = proceed_the_grid(passage_embedding, "batch", 0)
     local_questions = lax.dynamic_slice_in_dim(
         question_embedding, enc_index * half_count, half_count, 0
     )

time: 920 us -> 969 us (1.053)
  starting transfers between devices: 6.67 us -> 38.1 us
  local copies, waits for them, and re-layouts: 115 us -> 137 us
  blocking collectives: 143 us -> 121 us
  waiting for transfers between devices: 358 us -> 375 us
    ppermute x0 -> x15, starting transfers between devices: none -> 31.4 us  [the longest x7 31.3 us: proceed_the_grid(): w2.append(jax.lax.ppermute(w2[-1] if w2 else incoming_x, axis_tag, copies))]
    all_gather x1 -> x0, blocking collectives: 22.7 us -> none  [shards(): lax.all_gather(passage_embedding, 'batch', axis=0, tiled=True)]
    unnamed x154 -> x183, local copies, waits for them, and re-layouts: 51.5 us -> 70.4 us
    ppermute x0 -> x15, waiting for transfers between devices: none -> 14.9 us  [the longest x8 14.3 us: proceed_the_grid(): jax.lax.ppermute(x_new[-1] if x_new else incoming_x, axis_tag, trail)]
  transfers between devices with their start and end apart: 12 -> 27, of which waited for: 6 -> 17; matrix products, arithmetic and copies ran while one was open for 20% -> 21% of each run, Pallas kernels for 0% -> 0%
where the time goes in v1:
time: 969 us; the launch traced here: 958 us
  waiting for transfers between devices  375 us (39%)
  matrix products  189 us (20%)
  local copies, waits for them, and re-layouts  137 us (14%)
  blocking collectives  121 us (12%)
  other arithmetic  77.6 us (8%)
  starting transfers between devices  38.1 us (4%)
  between operations  19.1 us (2%)
    unnamed x2, blocking collectives  121 us
    reduce_scatter x1, waiting for transfers between devices, shards(): lax.psum_scatter(gradient_contraction, 'batch', scatter_dimension=0, tile...  114 us
    reduce_scatter x1, waiting for transfers between devices, shards(): lax.psum_scatter(gradient_expansion, 'batch', scatter_dimension=0, tiled=...  114 us
    unnamed x183, local copies, waits for them, and re-layouts  70.4 us
    reduce_scatter x1, waiting for transfers between devices, shards(): lax.psum_scatter(gradient_projection, 'batch', scatter_dimension=0, tiled...  64.9 us
    reduce_scatter x1, waiting for transfers between devices, shards(): lax.psum_scatter(jnp.einsum('qs,qd->sd', logits_gradient, local_questions...  54.4 us
    dot_general x1, matrix products, shards(): jnp.dot(first_low, expand_matrix, preferred_element_type=FLOAT_KIND)  35.9 us
    ppermute x7, starting transfers between devices, proceed_the_grid(): w2.append(jax.lax.ppermute(w2[-1] if w2 else incoming_x, axis_tag, copies))  31.3 us
  transfers between devices with their start and end apart: 27, of which 17 were waited for; matrix products, arithmetic and copies ran while one was open for 21% of the time, Pallas kernels for 0%

profile of v1, /device:TPU:0, one launch (start us, length us, event | category | flops | bytes accessed | tf_op | source)
XLA Modules:
  0.0 957.6 jit_solution(12947716319518690231)
XLA Ops:
  14.7 7.3 add_convert_fusion.1
  22.0 6.6 copy.99
  28.6 8.8 reshape.288
  37.4 5.4 slice_bitcast_fusion
  47.2 26.3 %while.26 = (s32[]{:T(128)}, bf16[2,512,12,64]{1,3,2,0:T(8,128)(2,1)}, f32[2,12,512,1]{2,1,3,0:T(8,128)}, bf16[2,512,12,64]{1,3,2,0:T(8,128)(2,1)}, s32[2,512]{1...) while((s32[]{:T(128)}, ...), condition=%wide.region_3.4_spmd, body=%wide.region_0.3_spmd.sunk | while | flops 840558592 | bytes 43204736 | solution.py:188
  55.2 5.1 fusion.138
  68.2 5.1 fusion.138
  81.7 35.9 %multiply_convert_fusion.1 = (bf16[1024,3072]{1,0:T(8,128)(2,1)}, f32[1024,3072]{1,0:T(8,128)}, f32[1024,3072]{1,0:T(8,128)}) fusion(f32[3072]{0:T(1024)S(1)} %bitcast.264, bf16[1,768,3072]{2,1,0:T(8,128)(2,1)S(1)} %bitcast.270, f32[1024,768]{0,1:T(8,128)S(1)} %get-tuple-element.312, f32[768]{0:T(1024)S(1)} %get-tuple-element.324, ...), kind=kOutput, calls=%fused_computation.64 | convolution fusion | flops 5043388416 | bytes 39348224 | tf_op jit(solution)/shard_map/dot_general | solution.py:195
  117.7 8.1 fusion.101
  127.7 4.3 collective-permute-start
  133.9 5.9 collective-permute-done.1
  139.9 4.4 collective-permute-start.9
  145.8 4.5 collective-permute-start.10
  151.8 4.4 collective-permute-start.11
  157.8 4.5 collective-permute-start.12
  164.4 4.4 collective-permute-start.13
  170.6 4.5 collective-permute-start.14
  179.5 4.4 collective-permute-start.15
  211.4 54.4 %reduce-scatter.8.cloned.1.call-done = f32[16,768]{1,0:T(8,128)} async-done(((f32[256,768]{1,0:T(8,128)}), f32[16,768]{1,0:T(8,128)}) %reduce-scatter.8.cloned.1.call-update) | async-done | bytes 49168 | tf_op jit(solution)/shard_map/reduce_scatter | solution.py:225
  275.3 5.8 multiply_reduce_fusion.1
  284.2 19.1 %convert_reduce_fusion = (f32[3072]{0:T(1024)}, bf16[1024,3072]{1,0:T(8,128)(2,1)}) fusion(f32[1024,3072]{1,0:T(8,128)} %get-tuple-element.299, bf16[1024,768]{0,1:T(8,128)(2,1)} %get-tuple-element.289, bf16[1,3072,768]{2,1,0:T(8,128)(2,1)} %param.32, f32[1024,3072]{1,0:T(8,128)} %get-tuple-element.313, f32[3072]{0:T(1024)S(1)} %bitcast.265), kind=kOutput, calls=%fused_computation.62 | convolution fusion | flops 4885312512 | bytes 37773312 | tf_op jit(solution)/shard_map/td,fd->tf/dot_general | solution.py:250
  303.4 11.0 %multiply_reduce_fusion.2 = (f32[768]{0:T(1024)}, f32[1024]{0:T(1024)S(1)}, f32[768]{0:T(1024)}, f32[1024,768]{0,1:T(8,128)S(1)}) fusion(f32[1024,768]{0,1:T(8,128)S(1)} %copy-done.9, f32[1024]{0:T(1024)S(1)} %copy-done.53, f32[1024]{0:T(1024)S(1)} %copy-done.37, f32[768]{0:T(1024)S(1)} %copy-done.50, bf16[1024,3072]{1,0:T(8,128)(2,1)} %get-tuple-element.323, ...), kind=kOutput, calls=%fused_computation.100 | convolution fusion | flops 4839699456 | bytes 20472832 | tf_op jit(solution)/shard_map/tf,df->td/dot_general | solution.py:259
  321.7 4.3 convolution_convert_fusion
  328.7 3.8 reshape.292
  335.5 53.4 %while.27 = (s32[]{:T(128)}, bf16[2,512,12,64]{1,3,2,0:T(8,128)(2,1)}, bf16[2,512,12,64]{1,3,2,0:T(8,128)(2,1)}, bf16[2,512,12,64]{1,3,2,0:T(8,128)(2,1)}, bf16[...) while((s32[]{:T(128)}, ...), condition=%wide.region_17.18_spmd, body=%wide.region_15.17_spmd.sunk | while | flops 2061494272 | bytes 156175728 | solution.py:272
  339.8 3.9 bitcast_dynamic-update-slice_fusion.11
  343.8 6.8 multiply_reduce_fusion.8
  350.6 7.2 multiply_convert_fusion.6
  366.6 3.9 bitcast_dynamic-update-slice_fusion.11
  370.5 6.8 multiply_reduce_fusion.8
  377.4 7.1 multiply_convert_fusion.6
  388.9 5.0 convert_reduce_fusion.1
  393.9 9.4 copy.112
  403.3 4.0 copy.127
  409.4 5.8 convolution_bitcast_fusion
  415.3 8.0 copy.124
  423.3 9.9 %fusion.105 = f32[3072,768]{1,0:T(8,128)} fusion(bf16[1024,3072]{1,0:T(8,128)(2,1)} %get-tuple-element.298, bf16[1024,768]{0,1:T(8,128)(2,1)} %get-tuple-element.289), kind=kOutput, calls=%fused_computation.221 | convolution fusion | flops 4831838208 | bytes 17301504 | tf_op jit(solution)/shard_map/tf,td->fd/dot_general | solution.py:247
  434.0 11.3 %fusion.92 = f32[768,3072]{1,0:T(8,128)} fusion(bf16[1024,3072]{1,0:T(8,128)(2,1)} %get-tuple-element.323, f32[1024,768]{0,1:T(8,128)} %copy-done.8, f32[768]{0:T(1024)S(1)} %copy-done.63, f32[768]{0:T(1024)S(1)} %copy-done.51, f32[1024]{0:T(1024)S(1)} %copy-done.54, f32[1024]{0:T(1024)S(1)} %copy-done.38), kind=kOutput, calls=%fused_computation.211 | convolution fusion | flops 4835770368 | bytes 18888704 | tf_op jit(solution)/shard_map/td,tf->df/dot_general | solution.py:256
  447.0 64.9 %reduce-scatter.16.cloned.1.call-done = f32[48,2304]{1,0:T(8,128)} async-done(((f32[768,2304]{1,0:T(8,128)}), f32[48,2304]{1,0:T(8,128)}) %reduce-scatter.16.cloned.1.call-update) | async-done | bytes 442384 | tf_op jit(solution)/shard_map/reduce_scatter | solution.py:291
  513.7 114.2 %reduce-scatter.14.cloned.1.call-done = f32[192,768]{1,0:T(8,128)} async-done(((f32[3072,768]{1,0:T(8,128)}), f32[192,768]{1,0:T(8,128)}) %reduce-scatter.14.cloned.1.call-update) | async-done | bytes 589840 | tf_op jit(solution)/shard_map/reduce_scatter | solution.py:299
  629.8 113.7 %reduce-scatter.12.cloned.1.call-done = f32[48,3072]{1,0:T(8,128)} async-done(((f32[768,3072]{1,0:T(8,128)}), f32[48,3072]{1,0:T(8,128)}) %reduce-scatter.12.cloned.1.call-update) | async-done | bytes 589840 | tf_op jit(solution)/shard_map/reduce_scatter | solution.py:297
  758.8 62.2 %all-reduce.16 = (bf16[1536]{0:T(1024)(128)(2,1)}, bf16[768]{0:T(1024)(128)(2,1)}, bf16[768]{0:T(1024)(128)(2,1)}, bf16[768]{0:T(1024)(128)(2,1)}, bf16[768]{0:T...) all-reduce(f32[1536]{0:T(1024)S(1)} %pad_maximum_fusion.2, ...), channel_id=4, replica_groups=mesh['enc'=2,'batch'=16] {'batch'}, use_global_device_ids=true, to_apply=%region_20.21.clone | all-reduce | flops 9216 | bytes 55296
  837.3 58.6 %all-reduce.17 = (bf16[1536]{0:T(1024)(128)(2,1)}, bf16[768]{0:T(1024)(128)(2,1)}, bf16[768]{0:T(1024)(128)(2,1)}, bf16[768]{0:T(1024)(128)(2,1)}, bf16[768]{0:T...) all-reduce(bf16[1536]{0:T(1024)(128)(2,1)S(1)} %dynamic-update-slic, ...), channel_id=1, replica_groups=mesh['enc'=2,'batch'=16] {'batch'}, use_global_device_ids=true, to_apply=%add | all-reduce | flops 9216 | bytes 36864
  906.1 8.0 add_bitcast_fusion
  920.4 5.5 bitcast_convert_fusion.2
  925.9 6.9 bitcast_convert_fusion
  932.8 10.4 %all-gather.9.cloned.1.call-done = bf16[768,3072]{1,0:T(8,128)(2,1)} async-done(((bf16[48,3072]{1,0:T(8,128)(2,1)}), bf16[768,3072]{1,0:T(8,128)(2,1)}) %all-gather.9.cloned.1.call-update) | async-done | bytes 4718608 | tf_op jit(solution)/shard_map/all_gather | solution.py:323
  943.3 7.4 bitcast_convert_fusion.1
  (363 shorter events, 174.5 us)
Async XLA Ops:
  7.2 258.6 %reduce-scatter.8.cloned.1.call-start = ((), (), s32[]{:S(2)}) async-start(), calls=%async_computation.5 | async-start | bytes 835584 | tf_op jit(solution)/shard_map/reduce_scatter | solution.py:225
  77.2 40.4 %slice-start = ((s8[4718592]{0:T(1024)(128)(4,1)}), s8[4194304]{0:T(1024)(128)(4,1)S(1)}, s32[]{:S(2)}) async-start(s8[4718592]{0:T(1024)(128)(4,1)} %bitcast.267), calls=%async_computation.14 | async-start | bytes 8388608
  78.9 38.7 %copy-start.8 = (f32[1024,768]{0,1:T(8,128)}, f32[1024,768]{0,1:T(8,128)S(1)}, u32[]{:S(2)}) copy-start(f32[1024,768]{0,1:T(8,128)S(1)} %get-tuple-element.312) | copy-start | bytes 9437188
  79.0 38.6 %copy-start.36 = (f32[1024]{0:T(1024)}, f32[1024]{0:T(1024)S(1)}, u32[]{:S(2)}) copy-start(f32[1024]{0:T(1024)S(1)} %broadcast_multiply_fusion.1) | copy-start | bytes 12292
  81.6 36.1 %copy-start.52 = (f32[1024]{0:T(1024)}, f32[1024]{0:T(1024)S(1)}, u32[]{:S(2)}) copy-start(f32[1024]{0:T(1024)S(1)} %fusion.85) | copy-start | bytes 12292
  81.6 36.0 %copy-start.49 = (f32[768]{0:T(1024)}, f32[768]{0:T(1024)S(1)}, u32[]{:S(2)}) copy-start(f32[768]{0:T(1024)S(1)} %get-tuple-element.325) | copy-start | bytes 9220
  81.6 36.0 %copy-start.62 = (f32[768]{0:T(1024)}, f32[768]{0:T(1024)S(1)}, u32[]{:S(2)}) copy-start(f32[768]{0:T(1024)S(1)} %get-tuple-element.324) | copy-start | bytes 9220
  81.7 36.0 %copy-start.64 = (f32[768]{0:T(1024)S(1)}, f32[768]{0:T(1024)}, u32[]{:S(2)}) copy-start(f32[768]{0:T(1024)} %convert_reduce_fusion.6) | copy-start | bytes 9220
  81.7 36.0 %slice-start.1 = ((s8[4718592]{0:T(1024)(128)(4,1)}), s8[524288]{0:T(1024)(128)(4,1)S(1)}, s32[]{:S(2)}) async-start(s8[4718592]{0:T(1024)(128)(4,1)} %bitcast.267), calls=%async_computation.15 | async-start | bytes 1048576
  125.9 155.2 %copy-start.23 = (f32[1024]{0:T(1024)}, f32[1024]{0:T(1024)S(1)}, u32[]{:S(2)}) copy-start(f32[1024]{0:T(1024)S(1)} %broadcast_multiply_fusion) | copy-start | bytes 12292
  125.9 37.9 %copy-start.71 = (s32[16]{0:T(128)S(1)}, s32[16]{0:T(128)}, u32[]{:S(2)}) copy-start(s32[16]{0:T(128)} %param.38) | copy-start | bytes 196
  126.9 154.2 %copy-start.27 = (f32[1024]{0:T(1024)}, f32[1024]{0:T(1024)S(1)}, u32[]{:S(2)}) copy-start(f32[1024]{0:T(1024)S(1)} %fusion.86) | copy-start | bytes 12292
  126.9 80.3 %copy-start.29 = (f32[768]{0:T(1024)}, f32[768]{0:T(1024)S(1)}, u32[]{:S(2)}) copy-start(f32[768]{0:T(1024)S(1)} %get-tuple-element.327) | copy-start | bytes 9220
  126.9 80.3 %copy-start.34 = (f32[768]{0:T(1024)}, f32[768]{0:T(1024)S(1)}, u32[]{:S(2)}) copy-start(f32[768]{0:T(1024)S(1)} %get-tuple-element.326) | copy-start | bytes 9220
  127.7 6.1 collective-permute-start
  133.8 6.0 collective-permute-start.1
  139.8 5.9 collective-permute-start.2
  139.9 6.0 collective-permute-start.9
  145.8 5.9 collective-permute-start.3
  145.8 6.0 collective-permute-start.10
  151.8 5.9 collective-permute-start.4
  151.8 5.9 collective-permute-start.11
  157.7 6.1 collective-permute-start.5
  157.8 6.6 collective-permute-start.12
  163.8 6.4 collective-permute-start.6
  164.4 6.2 collective-permute-start.13
  170.1 6.3 collective-permute-start.7
  170.6 8.9 collective-permute-start.14
  176.4 7.6 collective-permute-start.8
  179.5 24.6 %collective-permute-start.15 = (bf16[16,768]{1,0:T(8,128)(2,1)}, bf16[16,768]{1,0:T(8,128)(2,1)S(1)}, u32[]{:S(2)}, u32[]{:S(2)}) collective-permute-start(bf16[16,768]{1,0:T(8,128)(2,1)} %collective-permute-done.14), channel_id=1, source_target_pairs={{1,0},{2,1},{3,2},{4,3},{5,4},{6,5},{7,6},{8,7},{9,8},{10,9},{11,1... | collective-permute-start | bytes 73736 | tf_op jit(solution)/shard_map/ppermute | solution.py:35
  211.3 234.0 %reduce-scatter.10.cloned.1.call-start = ((), (), s32[]{:S(2)}) async-start(), calls=%async_computation.7 | async-start | bytes 2506752 | tf_op jit(solution)/shard_map/reduce_scatter | solution.py:293
  267.2 8.1 collective-permute-start.16
  270.6 4.0 collective-permute-start.17
  284.2 19.2 %copy-start.9 = (f32[1024,768]{0,1:T(8,128)S(1)}, f32[1024,768]{0,1:T(8,128)}, u32[]{:S(2)}) copy-start(f32[1024,768]{0,1:T(8,128)} %copy-done.8) | copy-start | bytes 9437188
  284.2 19.2 %copy-start.37 = (f32[1024]{0:T(1024)S(1)}, f32[1024]{0:T(1024)}, u32[]{:S(2)}) copy-start(f32[1024]{0:T(1024)} %copy-done.36) | copy-start | bytes 12292
  284.2 19.1 %copy-start.50 = (f32[768]{0:T(1024)S(1)}, f32[768]{0:T(1024)}, u32[]{:S(2)}) copy-start(f32[768]{0:T(1024)} %copy-done.49) | copy-start | bytes 9220
  284.2 19.1 %copy-start.53 = (f32[1024]{0:T(1024)S(1)}, f32[1024]{0:T(1024)}, u32[]{:S(2)}) copy-start(f32[1024]{0:T(1024)} %copy-done.52) | copy-start | bytes 12292
  335.4 176.5 %reduce-scatter.16.cloned.1.call-start = ((), (), s32[]{:S(2)}) async-start(), calls=%async_computation.13 | async-start | bytes 7520256 | tf_op jit(solution)/shard_map/reduce_scatter | solution.py:291
  423.3 204.6 %reduce-scatter.14.cloned.1.call-start = ((), (), s32[]{:S(2)}) async-start(), calls=%async_computation.11 | async-start | bytes 10027008 | tf_op jit(solution)/shard_map/reduce_scatter | solution.py:299
  433.3 310.2 %reduce-scatter.12.cloned.1.call-start = ((), (), s32[]{:S(2)}) async-start(), calls=%async_computation.9 | async-start | bytes 10027008 | tf_op jit(solution)/shard_map/reduce_scatter | solution.py:297
  445.3 305.3 %copy-start.24 = (f32[1024]{0:T(1024)S(1)}, f32[1024]{0:T(1024)}, u32[]{:S(2)}) copy-start(f32[1024]{0:T(1024)} %copy-done.23) | copy-start | bytes 12292
  445.3 305.3 %copy-start.28 = (f32[1024]{0:T(1024)S(1)}, f32[1024]{0:T(1024)}, u32[]{:S(2)}) copy-start(f32[1024]{0:T(1024)} %copy-done.27) | copy-start | bytes 12292
  445.3 305.3 %copy-start.31 = (f32[768]{0:T(1024)S(1)}, f32[768]{0:T(1024)}, u32[]{:S(2)}) copy-start(f32[768]{0:T(1024)} %copy-done.29) | copy-start | bytes 9220
  445.3 305.3 %copy-start.35 = (f32[768]{0:T(1024)S(1)}, f32[768]{0:T(1024)}, u32[]{:S(2)}) copy-start(f32[768]{0:T(1024)} %copy-done.34) | copy-start | bytes 9220
  445.3 472.3 %all-gather.7.cloned.1.call-start = ((), (), s32[]{:S(2)}) async-start(), calls=%async_computation.8 | async-start | bytes 1253376 | tf_op jit(solution)/shard_map/all_gather | solution.py:311
  447.0 473.5 %all-gather.5.cloned.1.call-start = ((), (), s32[]{:S(2)}) async-start(), calls=%async_computation.6 | async-start | bytes 3760128 | tf_op jit(solution)/shard_map/all_gather | solution.py:305
  513.7 412.3 %all-gather.11.cloned.1.call-start = ((), (), s32[]{:S(2)}) async-start(), calls=%async_computation.12 | async-start | bytes 5013504 | tf_op jit(solution)/shard_map/all_gather | solution.py:329
  629.7 313.5 %all-gather.9.cloned.1.call-start = ((), (), s32[]{:S(2)}) async-start(), calls=%async_computation.10 | async-start | bytes 5013504 | tf_op jit(solution)/shard_map/all_gather | solution.py:323
  (65 other events, 238.5 us)
Sparse Core Ops, SparseCore 0:
  211.5 54.2 reduce-scatter.7
  335.5 61.0 reduce-scatter.9
  423.4 88.4 reduce-scatter.15
  517.0 110.8 reduce-scatter.13
  632.4 111.0 reduce-scatter.11
  745.9 38.3 all-gather.6
  786.8 45.9 all-gather.4
  835.3 52.7 all-gather.10
  891.2 52.0 all-gather.8
